TPU v7x, 512 devices: a whole 4x4x16 slice. The times are simulated.
512 devices in a mesh: leaf: 8 (over x, core), row: 8 (over y, z_hi), col: 8 (over z_lo).
Axes of the slice: x: 4, y: 4, z: 16 (z_hi: 2, z_lo: 8; z = z_hi * 8 + z_lo), core: 2. Of those that a mesh axis runs over, the one named last changes fastest.
Arguments:
- child_front: float32 [8, 4096, 4096], P('leaf', 'row', 'col'), as said below
- parent_front: bfloat16 [8192, 32768], P('row', ('leaf', 'col')), as said below
- block_map: int32 [8, 30], replicated, may hold values from 0 to 63, as said below
Outputs:
- child_panel_t: float32 [8, 256, 4096], P('leaf', 'col', 'row')
- parent_panel_t: float32 [1024, 8192], P(('leaf', 'col'), 'row')
- parent_update: float32 [8192, 32768], P('row', ('leaf', 'col'))
Inputs may be any that keep to these rules, and one draw needn't show every extreme that they name: `child_front`: every child front is symmetric positive definite. `parent_front`: every parent front (each block of 8192 columns) is symmetric positive definite. `block_map`: in each row the entries are distinct. Of the contribution blocks that one device of a child's grid holds in its rows, at most 1 go to parent blocks whose rows one index of row holds; of those it holds in its columns, at most 1 go to parent blocks whose columns are held by one index of col, counting both leaves of the pair together; of all contribution blocks of one child, at most 4 go to parent blocks whose rows one index of row holds. All three bounds are reached.
All inputs are finite; a program needn't handle non-finite values.
Results may differ from a plain program's by a relative error of at most 0.0003.
Values sent between devices are 32-bit elements; how exact they have to be, the bound alone decides.
No kernel may reach another device: no remote copies, remote signals or barrier semaphores. Data moves between devices by JAX's collectives and lax.ppermute only.
A program may use at most 64 MiB of HBM per device.

v0:
```python
import jax
import jax.numpy as jnp
from jax import lax
from jax.sharding import PartitionSpec as P

BLK = 128


def from_partner(value, axis, bit):
    mask = 2**bit
    pairs = [(source, source ^ mask) for source in range(lax.axis_size(axis))]
    return lax.ppermute(value, axis, pairs)


def from_root(value, axis, source):
    kept = jnp.where(lax.axis_index(axis) == source, value, 0).astype(value.dtype)
    return lax.psum(kept, axis)


def pair_swap(values):
    return from_partner(values, "leaf", 0)


def one_hot(values, size):
    return (values[:, None] == jnp.arange(size)[None, :]).astype(jnp.float32)


def factor_panel(front_block, panel_width, row_start, col_start, paired):
    precise_setting = lax.Precision.HIGHEST
    panel_slab = from_root(front_block[:, :panel_width], "col", 0)
    if paired:
        partner = pair_swap(panel_slab)
        panel_slab = jnp.where(lax.axis_index("leaf") % 2 == 0, panel_slab, partner)
    block_cols = front_block.shape[1]
    joined = jnp.concatenate((front_block[:panel_width], panel_slab[:panel_width]), axis=1)
    joined = from_root(joined, "row", 0)
    top_block = joined[:, :block_cols]
    diagonal_block = joined[:, block_cols:]
    lower_factor = jnp.linalg.cholesky(diagonal_block)
    identity = jnp.eye(panel_width, dtype=jnp.float32)
    inverse_factor = jax.scipy.linalg.solve_triangular(lower_factor, identity, lower=True)
    rows_factor = jnp.dot(panel_slab, inverse_factor.T, precision=precise_setting)
    cols_factor = jnp.dot(inverse_factor, top_block, precision=precise_setting)
    update = jnp.dot(rows_factor, cols_factor, precision=precise_setting)
    row_ids = row_start + jnp.arange(front_block.shape[0])
    col_ids = col_start + jnp.arange(block_cols)
    keep_mask = (row_ids[:, None] >= panel_width) & (col_ids[None, :] >= panel_width)
    schur_part = jnp.where(keep_mask, front_block - update, jnp.float32(0.0))
    return (rows_factor, schur_part)


def shards(child_front, parent_front, block_map):
    leaf_id = lax.axis_index("leaf")
    row_id = lax.axis_index("row")
    col_id = lax.axis_index("col")
    row_count = lax.axis_size("row")
    col_count = lax.axis_size("col")
    precise_setting = lax.Precision.HIGHEST
    child_block = child_front[0]
    child_rows, child_cols = child_block.shape
    panel_width = child_cols // 2
    rows_factor, contribution = factor_panel(
        child_block, panel_width, row_id * child_rows, col_id * child_cols, False
    )
    out_width = panel_width // col_count
    child_out = lax.dynamic_slice_in_dim(rows_factor, col_id * out_width, out_width, 1).T[None]
    parent_rows, parent_cols = parent_front.shape
    parent_order = parent_rows * row_count
    row_span = parent_rows // BLK
    col_span = parent_cols // BLK
    row_blocks = child_rows // BLK
    col_blocks = child_cols // BLK
    cap_rows = max(1, row_blocks // row_count)
    cap_cols = max(1, col_blocks // col_count)
    own_map = lax.dynamic_index_in_dim(block_map, leaf_id, 0, keepdims=False)
    block_count = own_map.shape[0]
    block_ids = jnp.arange(block_count)
    global_ids = panel_width + block_ids * BLK
    src_row = global_ids // child_rows
    src_col = global_ids // child_cols
    dst_row = own_map // row_span
    owner_col = own_map // col_span
    dst_col = owner_col % col_count
    dst_half = owner_col // col_count
    earlier = block_ids[None, :] < block_ids[:, None]
    rank_row = jnp.sum(
        earlier & (src_row[None, :] == src_row[:, None]) & (dst_row[None, :] == dst_row[:, None]),
        axis=1,
    )
    rank_col = jnp.sum(
        earlier & (src_col[None, :] == src_col[:, None]) & (dst_col[None, :] == dst_col[:, None]),
        axis=1,
    )
    local_rows = (global_ids - row_id * child_rows) // BLK
    local_cols = (global_ids - col_id * child_cols) // BLK
    row_pick = jnp.einsum(
        "k,kd,ka,kx->dax",
        (src_row == row_id).astype(jnp.float32),
        one_hot(dst_row, row_count),
        one_hot(rank_row, cap_rows),
        one_hot(local_rows, row_blocks),
        precision=precise_setting,
    )
    col_pick = jnp.einsum(
        "k,ke,kj,ky->ejy",
        (src_col == col_id).astype(jnp.float32),
        one_hot(dst_col, col_count),
        one_hot(rank_col, cap_cols),
        one_hot(local_cols, col_blocks),
        precision=precise_setting,
    )
    place_cols = jnp.einsum(
        "k,kh,ky,kc,kj->hycj",
        (dst_col == col_id).astype(jnp.float32),
        one_hot(dst_half, 2),
        one_hot(own_map % col_span, col_span),
        one_hot(src_col, col_count),
        one_hot(rank_col, cap_cols),
        precision=precise_setting,
    )
    strip_view = contribution.reshape(row_blocks, BLK, child_cols)
    strips = jnp.einsum("dax,xiw->daiw", row_pick, strip_view, precision=precise_setting)
    received_blocks = lax.all_to_all(
        strips.reshape(row_count, cap_rows * BLK, child_cols),
        "row",
        split_axis=0,
        concat_axis=0,
        tiled=True,
    )
    received_blocks = received_blocks.reshape(row_count, cap_rows, BLK, child_cols)
    on_this_row = (dst_row == row_id).astype(jnp.float32)
    rank_dest = jnp.sum(earlier & (dst_row[None, :] == dst_row[:, None]), axis=1)
    cap_incoming = -(-block_count // row_count)
    dense_selection = jnp.einsum(
        "c,cn,cw,cp->nwp",
        on_this_row,
        one_hot(rank_dest, cap_incoming),
        one_hot(src_row, row_count),
        one_hot(rank_row, cap_rows),
        precision=precise_setting,
    )
    squeezed_result = jnp.einsum(
        "byx,yxhq->bhq", dense_selection, received_blocks, precision=precise_setting
    )
    squeezed_result = squeezed_result.reshape(cap_incoming, BLK, col_blocks, BLK)
    sending = jnp.einsum("miyb,ejy->emijb", squeezed_result, col_pick, precision=precise_setting)
    landed = lax.all_to_all(
        sending.reshape(col_count, cap_incoming * BLK, cap_cols * BLK),
        "col",
        split_axis=0,
        concat_axis=0,
        tiled=True,
    )
    landed = landed.reshape(col_count, cap_incoming, BLK, cap_cols, BLK)
    place_rows = jnp.einsum(
        "k,kx,km->xm",
        on_this_row,
        one_hot(own_map % row_span, row_span),
        one_hot(rank_dest, cap_incoming),
        precision=precise_setting,
    )
    placed_rows = jnp.einsum("xm,cmijb->xcijb", place_rows, landed, precision=precise_setting)
    halves = jnp.einsum(
        "xcijb,hycj->hxiyb", placed_rows, place_cols, precision=precise_setting
    ).reshape(2, parent_rows, parent_cols)
    own_half = leaf_id % 2
    own_part = lax.dynamic_index_in_dim(halves, own_half, 0, keepdims=False)
    other_part = lax.dynamic_index_in_dim(halves, 1 - own_half, 0, keepdims=False)
    assembled = parent_front.astype(jnp.float32) + own_part + pair_swap(other_part)
    parent_width = parent_cols // 2
    col_start = own_half * (parent_order // 2) + col_id * parent_cols
    parent_factor, parent_schur = factor_panel(
        assembled, parent_width, row_id * parent_rows, col_start, True
    )
    share_width = parent_width // (2 * col_count)
    share_start = (own_half * col_count + col_id) * share_width
    parent_out = lax.dynamic_slice_in_dim(parent_factor, share_start, share_width, 1).T
    return (child_out, parent_out, parent_schur)


def solution(mesh):
    placed = (P("leaf", "row", "col"), P("row", ("leaf", "col")), P())
    return jax.shard_map(
        shards,
        mesh=mesh,
        in_specs=placed,
        out_specs=(P("leaf", "col", "row"), P(("leaf", "col"), "row"), P("row", ("leaf", "col"))),
        check_vma=False,
    )
```

profile of v0, /device:TPU:6, one launch (start us, length us, event | category | flops | bytes accessed | tf_op | source)
XLA Modules:
  0.0 1079.2 jit_solution(1554957028383324433)
XLA Ops:
  7.2 1.6 copy.64
  8.8 0.8 slice_select_fusion.1
  9.7 0.7 and_select_fusion.4
  10.5 128.7 %all-reduce.6.cloned.1.call-done = f32[512,256]{0,1:T(8,128)} async-done(((f32[512,256]{0,1:T(8,128)}), f32[512,256]{0,1:T(8,128)}) %all-reduce.6.cloned.1.call-update) | async-done | bytes 524304 | tf_op jit(solution)/shard_map/psum | solution.py:17
  139.3 1.0 slice.92
  140.3 0.9 maximum_select_fusion
  141.8 207.1 %all-reduce.8.cloned.1.call-done = f32[256,768]{0,1:T(8,128)} async-done(((f32[256,768]{0,1:T(8,128)}), f32[256,768]{0,1:T(8,128)}) %all-reduce.8.cloned.1.call-update) | async-done | bytes 786448 | tf_op jit(solution)/shard_map/psum | solution.py:17
  348.8 1.0 slice.93
  349.9 1.0 fusion.23
  350.9 11.7 %cholesky.130 = f32[128,128]{1,0:T(8,128)S(1)} custom-call(f32[128,128]{1,0:T(8,128)S(1)} %cholesky.194), custom_call_target="Cholesky" | custom-call | tf_op jit(solution)/shard_map/jit(cholesky)/cholesky | solution.py:39
  362.7 9.8 custom-call.13
  373.0 11.7 %cholesky.147 = f32[128,128]{1,0:T(8,128)S(1)} custom-call(f32[128,128]{1,0:T(8,128)S(1)} %convolution_subtract_fusion.4), custom_call_target="Cholesky" | custom-call | tf_op jit(solution)/shard_map/jit(cholesky)/cholesky | solution.py:39
  384.8 0.7 compare_reduce_fusion.2
  386.8 4.2 while.4
  387.6 1.4 bitcast_dynamic-update-slice_fusion.4
  389.6 1.4 bitcast_dynamic-update-slice_fusion.4
  391.0 19.7 %custom-call.14 = f32[2,128,128]{1,2,0:T(8,128)S(1)} custom-call(f32[2,128,128]{2,1,0:T(8,128)S(1)} %get-tuple-element.19), custom_call_target="InvertDiagBlocksLowerTriangular" | custom-call | tf_op jit(solution)/shard_map/jit(_solve_triangular)/triangular_solve | solution.py:41
  411.6 0.6 fusion.26
  412.3 0.6 fusion.20
  413.1 1.2 fusion.15
  414.6 0.6 copy.69
  415.2 2.3 fusion.82
  417.5 2.5 copy.70
  420.0 8.9 all-to-all-start
  429.5 79.5 %all-to-all-done = f32[8,128,512]{2,1,0:T(8,128)S(1)} async-done(((f32[8,128,512]{2,1,0:T(8,128)}), f32[8,128,512]{2,1,0:T(8,128)S(1)}, u32[]{:S(2)}, u32[]{:S(2)}) %all-to-all-start) | async-done | bytes 2097184 | tf_op jit(solution)/shard_map/all_to_all | solution.py:123
  509.0 2.8 fusion.12
  512.1 2.8 fusion.16
  515.0 1.7 copy.74
  516.7 13.0 %all-to-all-start.1 = ((f32[8,512,128]{2,1,0:T(8,128)}), f32[8,512,128]{2,1,0:T(8,128)S(1)}, u32[]{:S(2)}, u32[]{:S(2)}) async-start(f32[8,512,128]{2,1,0:T(8,128)} %copy.74), calls=%async_computation.1 | async-start | bytes 4194304 | tf_op jit(solution)/shard_map/all_to_all | solution.py:147
  530.4 95.4 %all-to-all-done.1 = f32[8,512,128]{2,1,0:T(8,128)S(1)} async-done(((f32[8,512,128]{2,1,0:T(8,128)}), f32[8,512,128]{2,1,0:T(8,128)S(1)}, u32[]{:S(2)}, u32[]{:S(2)}) %all-to-all-start.1) | async-done | bytes 2097184 | tf_op jit(solution)/shard_map/all_to_all | solution.py:147
  625.7 5.9 fusion.9
  631.7 8.4 fusion.3
  640.0 5.5 reshape.323
  645.5 4.0 constant_dynamic-slice_fusion.3
  649.5 2.9 copy.88
  652.4 2.1 collective-permute-start
  654.6 1.5 copy.67
  656.1 1.8 copy.87
  657.9 0.9 collective-permute-done
  658.8 2.8 fusion.8
  661.6 1.2 slice_select_fusion
  662.9 127.0 %all-reduce.10.cloned.1.call-done = f32[1024,256]{0,1:T(8,128)} async-done(((f32[1024,256]{0,1:T(8,128)}), f32[1024,256]{0,1:T(8,128)}) %all-reduce.10.cloned.1.call-update) | async-done | bytes 1048592 | tf_op jit(solution)/shard_map/psum | solution.py:17
  789.9 1.9 collective-permute-start.1
  791.8 2.8 collective-permute-done.1
  794.6 1.4 broadcast_select_fusion
  796.1 1.0 maximum_select_fusion.1
  797.1 1.5 dynamic-slice_bitcast_fusion.1
  798.6 204.2 %all-reduce.12.cloned.1.call-done = f32[256,768]{0,1:T(8,128)} async-done(((f32[256,768]{0,1:T(8,128)}), f32[256,768]{0,1:T(8,128)}) %all-reduce.12.cloned.1.call-update) | async-done | bytes 786448 | tf_op jit(solution)/shard_map/psum | solution.py:17
  1002.8 1.0 slice.98
  1003.9 1.0 fusion.22
  1004.9 11.7 %cholesky.164 = f32[128,128]{1,0:T(8,128)S(1)} custom-call(f32[128,128]{1,0:T(8,128)S(1)} %cholesky.197), custom_call_target="Cholesky" | custom-call | tf_op jit(solution)/shard_map/jit(cholesky)/cholesky | solution.py:39
  1016.7 9.8 custom-call.15
  1027.0 11.7 %cholesky.181 = f32[128,128]{1,0:T(8,128)S(1)} custom-call(f32[128,128]{1,0:T(8,128)S(1)} %convolution_subtract_fusion.3), custom_call_target="Cholesky" | custom-call | tf_op jit(solution)/shard_map/jit(cholesky)/cholesky | solution.py:39
  1038.7 0.6 compare_reduce_fusion.1
  1039.3 0.7 compare_reduce_fusion
  1041.2 4.0 while.5
  1042.1 1.3 bitcast_dynamic-update-slice_fusion.5
  1043.9 1.3 bitcast_dynamic-update-slice_fusion.5
  1045.2 19.7 %custom-call.16 = f32[2,128,128]{1,2,0:T(8,128)S(1)} custom-call(f32[2,128,128]{2,1,0:T(8,128)S(1)} %get-tuple-element.20), custom_call_target="InvertDiagBlocksLowerTriangular" | custom-call | tf_op jit(solution)/shard_map/jit(_solve_triangular)/triangular_solve | solution.py:41
  1065.8 1.1 fusion.25
  1066.9 0.6 dynamic-slice_bitcast_fusion
  1067.6 0.6 fusion.18
  1068.2 2.2 subtract_select_fusion
  1070.4 1.8 copy.81
  (79 shorter events, 8.6 us)
Async XLA Ops:
  7.2 132.1 %all-reduce.6.cloned.1.call-start = ((), (), s32[]{:S(2)}) async-start(), calls=%async_computation.2 | async-start | bytes 1048576 | tf_op jit(solution)/shard_map/psum | solution.py:17
  9.6 339.2 %all-reduce.8.cloned.1.call-start = ((), (), s32[]{:S(2)}) async-start(), calls=%async_computation.3 | async-start | bytes 1572864 | tf_op jit(solution)/shard_map/psum | solution.py:17
  350.9 60.7 %copy-start.5 = (f32[512,256]{0,1:T(8,128)S(1)}, f32[512,256]{0,1:T(8,128)}, u32[]{:S(2)}) copy-start(f32[512,256]{0,1:T(8,128)} %all-reduce.6.cloned.1.call-done) | copy-start | bytes 1572868
  373.0 39.2 %copy-start.4 = (f32[256,768]{0,1:T(8,128)S(1)}, f32[256,768]{0,1:T(8,128)}, u32[]{:S(2)}) copy-start(f32[256,768]{0,1:T(8,128)} %all-reduce.8.cloned.1.call-done) | copy-start | bytes 2359300
  412.2 0.8 copy-start.2
  420.0 88.9 %all-to-all-start = ((f32[8,128,512]{2,1,0:T(8,128)}), f32[8,128,512]{2,1,0:T(8,128)S(1)}, u32[]{:S(2)}, u32[]{:S(2)}) async-start(f32[8,128,512]{2,1,0:T(8,128)} %copy.70), calls=%async_computation | async-start | bytes 4194304 | tf_op jit(solution)/shard_map/all_to_all | solution.py:123
  516.7 109.0 %all-to-all-start.1 = ((f32[8,512,128]{2,1,0:T(8,128)}), f32[8,512,128]{2,1,0:T(8,128)S(1)}, u32[]{:S(2)}, u32[]{:S(2)}) async-start(f32[8,512,128]{2,1,0:T(8,128)} %copy.74), calls=%async_computation.1 | async-start | bytes 4194304 | tf_op jit(solution)/shard_map/all_to_all | solution.py:147
  529.7 260.1 %all-reduce.10.cloned.1.call-start = ((), (), s32[]{:S(2)}) async-start(), calls=%async_computation.4 | async-start | bytes 2097152 | tf_op jit(solution)/shard_map/psum | solution.py:17
  652.4 6.4 collective-permute-start
  661.6 130.2 %copy-start = (f32[1024,512]{0,1:T(8,128)}, f32[1024,512]{0,1:T(8,128)S(1)}, u32[]{:S(2)}) copy-start(f32[1024,512]{0,1:T(8,128)S(1)} %fusion.8) | copy-start | bytes 6291460
  662.8 340.0 %all-reduce.12.cloned.1.call-start = ((), (), s32[]{:S(2)}) async-start(), calls=%async_computation.5 | async-start | bytes 1572864 | tf_op jit(solution)/shard_map/psum | solution.py:17
  789.9 4.8 collective-permute-start.1
  794.6 1.5 slice-start
  1041.2 26.3 %copy-start.3 = (f32[256,768]{0,1:T(8,128)S(1)}, f32[256,768]{0,1:T(8,128)}, u32[]{:S(2)}) copy-start(f32[256,768]{0,1:T(8,128)} %all-reduce.12.cloned.1.call-done) | copy-start | bytes 2359300
  1065.5 2.7 copy-start.1
Sparse Core Ops, SparseCore 0:
  11.5 127.7 all-reduce.5
  143.1 205.7 all-reduce.7
  662.9 126.8 all-reduce.9
  797.2 205.5 all-reduce.11
where the time goes:
time: 1090 us; the launch traced here: 1080 us
  waiting for transfers between devices  846 us (78%)
  other arithmetic  119 us (11%)
  local copies, waits for them, and re-layouts  37.9 us (3%)
  matrix products  32.4 us (3%)
  starting transfers between devices  26.2 us (2%)
  between operations  17.3 us (2%)
    psum x4, waiting for transfers between devices, from_root(): return lax.psum(kept, axis)  667 us
    all_to_all x1, waiting for transfers between devices, shards(): lax.all_to_all(sending.reshape(col_count, cap_incoming * BLK, cap_cols *...  95.4 us
    all_to_all x1, waiting for transfers between devices, shards(): lax.all_to_all(strips.reshape(row_count, cap_rows * BLK, child_cols), 'ro...  79.5 us
    another operation x13, other arithmetic, factor_panel(): lower_factor = jnp.linalg.cholesky(diagonal_block)  68.5 us
    another operation x5, other arithmetic, factor_panel(): jax.scipy.linalg.solve_triangular(lower_factor, identity, lower=True)  39.4 us
  transfers between devices with their start and end apart: 8, of which 8 were waited for; matrix products, arithmetic and copies ran while one was open for 1% of the time, Pallas kernels for 0%

commit v1 on v0

--- a/solution.py
+++ b/solution.py
@@ -14,7 +14,7 @@
 
 def from_root(value, axis, source):
     kept = jnp.where(lax.axis_index(axis) == source, value, 0).astype(value.dtype)
-    return lax.psum(kept, axis)
+    return jnp.sum(lax.all_gather(kept, axis), axis=0)
 
 
 def pair_swap(values):

time: 1090 us -> 1190 us (1.092)
  the two profiles are of different devices: /device:TPU:6 before, /device:TPU:98 now
where the time goes in v1:
time: 1190 us; the launch traced here: 1180 us
  waiting for transfers between devices  941 us (79%)
  other arithmetic  136 us (11%)
  matrix products  37.4 us (3%)
  local copies, waits for them, and re-layouts  30.8 us (3%)
  between operations  17.4 us (1%)
  starting transfers between devices  13.7 us (1%)
    all_gather x4, waiting for transfers between devices, from_root(): return jnp.sum(lax.all_gather(kept, axis), axis=0)  761 us
    all_to_all x1, waiting for transfers between devices, shards(): lax.all_to_all(sending.reshape(col_count, cap_incoming * BLK, cap_cols *...  89.2 us
    all_to_all x1, waiting for transfers between devices, shards(): lax.all_to_all(strips.reshape(row_count, cap_rows * BLK, child_cols), 'ro...  83.6 us
    another operation x13, other arithmetic, factor_panel(): lower_factor = jnp.linalg.cholesky(diagonal_block)  69.3 us
    another operation x5, other arithmetic, factor_panel(): jax.scipy.linalg.solve_triangular(lower_factor, identity, lower=True)  41.9 us
  transfers between devices with their start and end apart: 8, of which 8 were waited for; matrix products, arithmetic and copies ran while one was open for 0% of the time, Pallas kernels for 0%

profile of v1, /device:TPU:98, one launch (start us, length us, event | category | flops | bytes accessed | tf_op | source)
XLA Modules:
  0.0 1176.8 jit_solution(3930161530986891701)
XLA Ops:
  7.2 1.9 slice_select_fusion.1
  9.2 1.1 slice.65
  10.3 99.7 %all-gather.11.cloned.1.call-done = f32[4096,256]{1,0:T(8,128)} async-done(((f32[512,256]{1,0:T(8,128)}), f32[4096,256]{1,0:T(8,128)}) %all-gather.11.cloned.1.call-update) | async-done | bytes 4194320 | tf_op jit(solution)/shard_map/all_gather | solution.py:17
  109.9 2.5 reduce_sum.63
  112.5 0.9 maximum_select_fusion
  113.5 0.7 and_select_fusion.4
  114.8 240.3 %all-gather.7.cloned.1.call-done = f32[8,256,768]{2,1,0:T(8,128)} async-done(((f32[1,256,768]{2,1,0:T(8,128)}), f32[8,256,768]{2,1,0:T(8,128)}) %all-gather.7.cloned.1.call-update) | async-done | bytes 6291472 | tf_op jit(solution)/shard_map/all_gather | solution.py:17
  355.1 3.2 reduce_sum.64
  358.6 11.7 cholesky.130
  370.4 9.8 custom-call.13
  380.7 11.7 cholesky.147
  392.4 0.7 compare_reduce_fusion.2
  394.6 4.5 while.4
  395.6 1.4 bitcast_dynamic-update-slice_fusion.4
  397.6 1.4 bitcast_dynamic-update-slice_fusion.4
  399.1 19.7 %custom-call.14 = f32[2,128,128]{1,2,0:T(8,128)S(1)} custom-call(f32[2,128,128]{2,1,0:T(8,128)S(1)} %get-tuple-element.19), custom_call_target="InvertDiagBlocksLowerTriangular" | custom-call | tf_op jit(solution)/shard_map/jit(_solve_triangular)/triangular_solve | solution.py:41
  420.9 1.1 fusion.15
  422.1 2.8 fusion.18
  424.9 2.5 copy.39
  427.4 3.6 all-to-all-start
  431.6 83.6 %all-to-all-done = f32[8,128,512]{2,1,0:T(8,128)S(1)} async-done(((f32[8,128,512]{2,1,0:T(8,128)}), f32[8,128,512]{2,1,0:T(8,128)S(1)}, u32[]{:S(2)}, u32[]{:S(2)}) %all-to-all-start) | async-done | bytes 2097184 | tf_op jit(solution)/shard_map/all_to_all | solution.py:123
  515.2 2.8 fusion.12
  518.4 2.8 fusion.16
  521.2 1.7 copy.43
  522.9 5.8 all-to-all-start.1
  529.3 89.2 %all-to-all-done.1 = f32[8,512,128]{2,1,0:T(8,128)S(1)} async-done(((f32[8,512,128]{2,1,0:T(8,128)}), f32[8,512,128]{2,1,0:T(8,128)S(1)}, u32[]{:S(2)}, u32[]{:S(2)}) %all-to-all-start.1) | async-done | bytes 2097184 | tf_op jit(solution)/shard_map/all_to_all | solution.py:147
  618.4 5.9 fusion.9
  624.4 8.4 fusion.3
  632.8 5.5 reshape.379
  638.2 1.9 dynamic-slice_bitcast_fusion
  640.1 1.9 collective-permute-start
  642.0 4.2 collective-permute-done
  646.3 2.8 fusion.8
  649.1 1.1 slice_select_fusion
  650.2 180.8 %all-gather.13.cloned.1.call-done = f32[8192,256]{1,0:T(8,128)} async-done(((f32[1024,256]{1,0:T(8,128)}), f32[8192,256]{1,0:T(8,128)}) %all-gather.13.cloned.1.call-update) | async-done | bytes 8388624 | tf_op jit(solution)/shard_map/all_gather | solution.py:17
  831.0 4.1 reduce_sum.68
  835.1 2.1 collective-permute-start.1
  837.3 2.5 collective-permute-done.1
  839.8 1.4 broadcast_select_fusion
  841.2 0.9 maximum_select_fusion.1
  842.2 1.5 dynamic-slice_bitcast_fusion.2
  843.7 240.2 %all-gather.9.cloned.1.call-done = f32[8,256,768]{2,1,0:T(8,128)} async-done(((f32[1,256,768]{2,1,0:T(8,128)}), f32[8,256,768]{2,1,0:T(8,128)}) %all-gather.9.cloned.1.call-update) | async-done | bytes 6291472 | tf_op jit(solution)/shard_map/all_gather | solution.py:17
  1083.9 4.1 reduce_sum.69
  1088.0 1.7 slice.94
  1089.7 1.8 copy.52
  1091.4 1.1 fusion.24
  1092.5 0.7 copy-done.5
  1093.2 11.7 cholesky.164
  1105.0 0.7 cholesky.189
  1105.7 9.8 custom-call.15
  1115.5 1.7 constant_dynamic-update-slice_fusion
  1117.2 1.1 convolution_subtract_fusion.3
  1118.3 11.7 cholesky.181
  1130.0 0.7 compare_reduce_fusion.1
  1133.2 1.7 select_select_fusion
  1134.9 6.1 while.5
  1135.2 0.6 fusion.106
  1135.8 2.3 bitcast_dynamic-update-slice_fusion.5
  1138.8 2.2 bitcast_dynamic-update-slice_fusion.5
  1141.0 0.6 copy-done.6
  1141.6 20.5 %custom-call.16 = f32[2,128,128]{1,2,0:T(8,128)S(1)} custom-call(f32[2,128,128]{2,1,0:T(8,128)} %copy-done.6), custom_call_target="InvertDiagBlocksLowerTriangular" | custom-call | tf_op jit(solution)/shard_map/jit(_solve_triangular)/triangular_solve | solution.py:41
  1162.5 1.1 convolution_subtract_fusion.1
  1163.9 1.1 fusion.27
  1166.2 3.6 subtract_select_fusion
  (78 shorter events, 10.4 us)
Async XLA Ops:
  7.2 102.8 %all-gather.11.cloned.1.call-start = ((), (), s32[]{:S(2)}) async-start(), calls=%async_computation.4 | async-start | bytes 4718592 | tf_op jit(solution)/shard_map/all_gather | solution.py:17
  9.1 346.0 %all-gather.7.cloned.1.call-start = ((), (), s32[]{:S(2)}) async-start(), calls=%async_computation.2 | async-start | bytes 7077888 | tf_op jit(solution)/shard_map/all_gather | solution.py:17
  394.6 26.3 %copy-start.2 = (f32[1,512,512]{2,1,0:T(8,128)S(1)}, f32[1,512,512]{2,1,0:T(8,128)}, u32[]{:S(2)}) copy-start(f32[1,512,512]{2,1,0:T(8,128)} %param.6) | copy-start | bytes 3145732
  420.3 1.8 copy-start.3
  427.4 87.7 %all-to-all-start = ((f32[8,128,512]{2,1,0:T(8,128)}), f32[8,128,512]{2,1,0:T(8,128)S(1)}, u32[]{:S(2)}, u32[]{:S(2)}) async-start(f32[8,128,512]{2,1,0:T(8,128)} %copy.39), calls=%async_computation | async-start | bytes 4194304 | tf_op jit(solution)/shard_map/all_to_all | solution.py:123
  522.9 95.6 %all-to-all-start.1 = ((f32[8,512,128]{2,1,0:T(8,128)}), f32[8,512,128]{2,1,0:T(8,128)S(1)}, u32[]{:S(2)}, u32[]{:S(2)}) async-start(f32[8,512,128]{2,1,0:T(8,128)} %copy.43), calls=%async_computation.1 | async-start | bytes 4194304 | tf_op jit(solution)/shard_map/all_to_all | solution.py:147
  528.6 302.4 %all-gather.13.cloned.1.call-start = ((), (), s32[]{:S(2)}) async-start(), calls=%async_computation.5 | async-start | bytes 9437184 | tf_op jit(solution)/shard_map/all_gather | solution.py:17
  638.2 8.0 copy-start.4
  640.1 6.2 collective-permute-start
  650.2 433.7 %all-gather.9.cloned.1.call-start = ((), (), s32[]{:S(2)}) async-start(), calls=%async_computation.3 | async-start | bytes 7077888 | tf_op jit(solution)/shard_map/all_gather | solution.py:17
  835.1 2.2 copy-start.1
  835.1 4.7 collective-permute-start.1
  1092.5 0.7 copy-start.5
  1141.0 0.7 copy-start.6
  1162.1 2.8 copy-start
Sparse Core Ops, SparseCore 0:
  10.7 99.2 all-gather.10
  113.7 241.3 all-gather.6
  650.3 180.6 all-gather.12
  842.3 241.5 all-gather.8
